TPU v7x, 32 devices: a whole 2x2x4 slice. The times are simulated.
32 devices in a mesh: tp: 8 (over y, x, core), dp: 4 (over z).
Axes of the slice: x: 2, y: 2, z: 4, core: 2. Of those that a mesh axis runs over, the one named last changes fastest.
Arguments:
- activations: bfloat16 [64, 512, 4096], P('dp', None, 'tp'), may hold values from -6 to 6
- query_output_cotangent: bfloat16 [64, 512, 4096], P('dp', None, 'tp'), may hold values from -6 to 6
- value_output_cotangent: bfloat16 [64, 512, 4096], P('dp', None, 'tp'), may hold values from -6 to 6
- lengths: int32 [64], P('dp'), may hold values from 1 to 512
- reducing_matrices_pair: bfloat16 [2, 4096, 128], P(None, 'tp'), may hold values from -0.09375 to 0.09375
- expanding_matrices_pair: bfloat16 [2, 128, 4096], P(None, None, 'tp'), may hold values from -0.5 to 0.5
- width_side_projections: bfloat16 [2, 4096, 128], P(None, 'tp'), may hold values from -0.09375 to 0.09375
- narrow_random_sketch: bfloat16 [128, 16], replicated, may hold values from -0.5 to 0.5
- projected_first_moment: float32 [8192], replicated, may hold values from -6 to 6
- projected_second_moment: float32 [8192], replicated, may hold values from 0.1 to 10
- targets: bfloat16 [1024, 8192], P('dp', 'tp'), may hold values from -6 to 6
Outputs:
- scores: float32 [64, 1024], P('dp', 'tp')
All inputs are finite; a program needn't handle non-finite values.
Results may differ from a plain program's by a relative error of at most 0.023.
Values may be sent and summed in bfloat16 or wider, within the bound.
A program may use at most 128 MiB of HBM per device.

v0:
```python
import math
import jax
import jax.numpy as jnp
from jax import lax
from jax.sharding import PartitionSpec as P


def compute_features(token_sums, token_mask, layout, rank_cols):
    wide_cols = (token_sums.shape[-1] - 4 * rank_cols) // 3
    bounds = [
        0,
        rank_cols,
        2 * rank_cols,
        2 * rank_cols + wide_cols,
        3 * rank_cols + wide_cols,
        3 * rank_cols + 2 * wide_cols,
        4 * rank_cols + 2 * wide_cols,
        4 * rank_cols + 3 * wide_cols,
    ]
    pieces = [token_sums[..., bounds[i] : bounds[i + 1]] for i in range(7)]
    down_q, down_v, input_side, back_q, output_q, back_v, output_v = pieces
    weights = token_mask[..., None]
    pattern = layout + "r," + layout + "k->erk"

    def outer_sum(left_side, right_side):
        return jnp.einsum(pattern, left_side, right_side, precision=lax.Precision.HIGHEST)

    stacked = jnp.stack(
        [
            outer_sum(back_q * weights, input_side),
            outer_sum(back_v * weights, input_side),
            outer_sum(down_q * weights, output_q),
            outer_sum(down_v * weights, output_v),
        ],
        axis=1,
    )
    return stacked.reshape(stacked.shape[0], -1)


def adam_update(features, first_moment, second_moment):
    mixed = 0.9 * first_moment + 0.1 * features
    spread = 0.999 * second_moment + 0.001 * features * features
    return mixed / (jnp.sqrt(spread) + 1e-08)


def combine_factors(reducing_matrices_pair, expanding_matrices_pair, narrow_random_sketch):
    attention_key_reducer = jnp.dot(
        reducing_matrices_pair[0], narrow_random_sketch, preferred_element_type=jnp.float32
    ).astype(jnp.bfloat16)
    value_down_factor = jnp.dot(
        reducing_matrices_pair[1], narrow_random_sketch, preferred_element_type=jnp.float32
    ).astype(jnp.bfloat16)
    query_up_factor = jnp.dot(
        expanding_matrices_pair[0].T, narrow_random_sketch, preferred_element_type=jnp.float32
    ).astype(jnp.bfloat16)
    value_up_factor = jnp.dot(
        expanding_matrices_pair[1].T, narrow_random_sketch, preferred_element_type=jnp.float32
    ).astype(jnp.bfloat16)
    return (attention_key_reducer, value_down_factor, query_up_factor, value_up_factor)


def body(
    activations,
    query_output_cotangent,
    value_output_cotangent,
    lengths,
    reducing_matrices_pair,
    expanding_matrices_pair,
    width_side_projections,
    narrow_random_sketch,
    projected_first_moment,
    projected_second_moment,
    targets,
):
    attention_key_reducer, value_down_factor, query_up_factor, value_up_factor = combine_factors(
        reducing_matrices_pair, expanding_matrices_pair, narrow_random_sketch
    )
    rank_cols = narrow_random_sketch.shape[1]
    w_left = jnp.concatenate(
        [attention_key_reducer, value_down_factor, width_side_projections[0]], axis=1
    )
    w_query = jnp.concatenate([query_up_factor, width_side_projections[1]], axis=1)
    w_value = jnp.concatenate([value_up_factor, width_side_projections[1]], axis=1)
    groups = lax.axis_size("tp")
    member = lax.axis_index("tp")
    local_ex = activations.shape[0]
    seq_len = activations.shape[1]
    feature_count = projected_first_moment.shape[0]
    positions = jnp.arange(seq_len, dtype=jnp.int32)
    token_mask = (positions[None, :] < lengths[:, None]).astype(jnp.float32)
    target_float = targets.astype(jnp.float32)
    target_sq = jnp.sum(target_float * target_float, axis=1)
    own_rows = local_ex // groups
    left_part = jnp.einsum("esd,dc->esc", activations, w_left, preferred_element_type=jnp.float32)
    right_q = jnp.einsum(
        "esd,dc->esc", query_output_cotangent, w_query, preferred_element_type=jnp.float32
    )
    right_v = jnp.einsum(
        "esd,dc->esc", value_output_cotangent, w_value, preferred_element_type=jnp.float32
    )
    token_sums = lax.psum_scatter(
        jnp.concatenate([left_part, right_q, right_v], axis=-1).astype(jnp.bfloat16),
        "tp",
        scatter_dimension=0,
        tiled=True,
    ).astype(jnp.float32)
    own_mask = lax.dynamic_slice_in_dim(token_mask, member * own_rows, own_rows, 0)
    features = compute_features(token_sums, own_mask, "es", rank_cols)
    update = adam_update(features, projected_first_moment, projected_second_moment)
    squares = jnp.sum(update * update, axis=1)
    target_total = lax.psum(target_sq, "tp")
    own_train = (update * lax.rsqrt(squares + 1e-06)[:, None]).astype(jnp.bfloat16)
    train_rows = lax.all_to_all(own_train, "tp", split_axis=1, concat_axis=0, tiled=True)
    unit_targets = (target_float * lax.rsqrt(target_total + 1e-06)[:, None]).astype(jnp.bfloat16)
    partial_scores = lax.dot_general(
        train_rows,
        lax.all_gather(unit_targets, "dp", axis=0, tiled=True),
        (((1,), (1,)), ((), ())),
        preferred_element_type=jnp.float32,
    )
    scores = lax.psum_scatter(
        partial_scores.astype(jnp.bfloat16), "tp", scatter_dimension=1, tiled=True
    ).astype(jnp.float32)
    return scores * math.sqrt(feature_count)


def solution(mesh):
    placed = (
        P("dp", None, "tp"),
        P("dp", None, "tp"),
        P("dp", None, "tp"),
        P("dp"),
        P(None, "tp", None),
        P(None, None, "tp"),
        P(None, "tp", None),
        P(),
        P(),
        P(),
        P("dp", "tp"),
    )
    return jax.shard_map(body, mesh=mesh, in_specs=placed, out_specs=P("dp", "tp"), check_vma=False)
```

profile of v0, /device:TPU:0, one launch (start us, length us, event | category | flops | bytes accessed | tf_op | source)
XLA Modules:
  0.0 158.5 jit_solution(14947241364090054816)
XLA Ops:
  7.4 0.0 copy-start
  7.4 0.0 reduce-scatter.5.cloned.1.call-start
  7.4 0.7 copy-done
  8.1 1.0 convolution_convert_fusion.1
  9.1 1.0 convolution_convert_fusion.2
  10.1 1.0 convolution_convert_fusion.3
  11.2 1.1 convolution_convert_fusion.4
  12.2 1.0 fusion.41
  13.2 0.1 copy.41
  13.4 0.1 copy.40
  13.5 0.0 copy-start.1
  13.5 6.4 %convert_bitcast_fusion.1 = bf16[16,512,144]{1,2,0:T(8,128)(2,1)S(1)} fusion(bf16[16,512,512]{2,1,0:T(8,128)(2,1)} %param.13, bf16[512,16]{0,1:T(8,128)(2,1)S(1)} %convolution_convert_fusion.1, bf16[512,128]{0,1:T(8,128)(2,1)S(1)} %bitcast.53), kind=kOutput, calls=%fused_computation.2 | convolution fusion | flops 1209434112 | bytes 10895360 | tf_op jit(solution)/shard_map/esd,dc->esc/dot_general | solution.py:98
  19.9 0.0 copy-done.1
  19.9 0.0 copy-start.2
  19.9 2.9 %convert_bitcast_fusion.2 = bf16[16,512,144]{1,2,0:T(8,128)(2,1)S(1)} fusion(bf16[16,512,512]{2,1,0:T(8,128)(2,1)S(1)} %copy-done.1, bf16[512,16]{0,1:T(8,128)(2,1)S(1)} %convolution_convert_fusion.2, bf16[512,128]{0,1:T(8,128)(2,1)S(1)} %bitcast.54), kind=kOutput, calls=%fused_computation.3 | convolution fusion | flops 1209434112 | bytes 10895360 | tf_op jit(solution)/shard_map/esd,dc->esc/dot_general | solution.py:95
  22.8 0.5 copy-done.2
  23.3 2.9 %convert_bitcast_fusion = bf16[16,512,160]{1,2,0:T(8,128)(2,1)S(1)} fusion(bf16[16,512,512]{2,1,0:T(8,128)(2,1)S(1)} %copy-done.2, bf16[512,128]{0,1:T(8,128)(2,1)S(1)} %bitcast.56, bf16[512,16]{0,1:T(8,128)(2,1)S(1)} %convolution_convert_fusion.3, bf16[512,16]{0,1:T(8,128)(2,1)S(1)} %convolution_convert_fusion.4), kind=kOutput, calls=%fused_computation.1 | convolution fusion | flops 1343979520 | bytes 11173888 | tf_op jit(solution)/shard_map/esd,dc->esc/dot_general | solution.py:94
  26.2 3.4 %pad_maximum_fusion = bf16[16,512,448]{1,2,0:T(8,128)(2,1)} fusion(bf16[16,512,144]{1,2,0:T(8,128)(2,1)S(1)} %convert_bitcast_fusion.1, bf16[16,512,144]{1,2,0:T(8,128)(2,1)S(1)} %convert_bitcast_fusion.2, bf16[16,512,160]{1,2,0:T(8,128)(2,1)S(1)} %convert_bitcast_fusion), kind=kLoop, calls=%fused_computation | loop fusion | flops 22020096 | bytes 14680064 | tf_op jit(solution)/shard_map/concatenate | solution.py:102
  29.5 0.0 copy-start.3
  29.5 0.0 reduce-scatter.5.cloned.1.call-update
  29.6 0.0 all-gather.2.cloned.1.call-start
  29.6 1.0 copy-done.3
  30.6 0.2 fusion
  30.7 15.1 %psum.7 = f32[256]{0:T(256)S(1)} all-reduce(f32[256]{0:T(256)S(1)} %fusion), channel_id=1, replica_groups=mesh['tp'=8,'dp'=4] {'tp'}, use_global_device_ids=true, to_apply=%region_3.0 | all-reduce | flops 256 | bytes 2048 | tf_op jit(solution)/shard_map/psum | solution.py:111
  45.9 1.0 fusion.1
  46.8 0.0 all-gather.2.cloned.1.call-update
  46.9 0.0 reduce-scatter.7.cloned.1.call-start
  46.9 0.0 copy-done.4
  47.0 0.0 copy-done.5
  47.0 0.0 copy-done.6
  47.0 0.1 dynamic-slice
  47.1 0.1 compare_convert_fusion
  47.2 52.2 %reduce-scatter.5.cloned.1.call-done = bf16[2,512,448]{1,2,0:T(8,128)(2,1)} async-done(((bf16[16,512,448]{1,2,0:T(8,128)(2,1)}), bf16[2,512,448]{1,2,0:T(8,128)(2,1)}) %reduce-scatter.5.cloned.1.call-update) | async-done | bytes 917520 | tf_op jit(solution)/shard_map/reduce_scatter | solution.py:101
  99.3 1.4 convert_element_type.39
  100.8 1.3 convolution_bitcast_fusion.3
  102.0 1.3 convolution_bitcast_fusion.2
  103.3 1.3 convolution_bitcast_fusion.1
  104.6 1.3 convolution_bitcast_fusion
  105.8 0.2 fusion.33
  106.0 0.1 fusion.32
  106.2 7.4 %all_to_all.16 = bf16[2,8,1024]{2,0,1:T(2,128)(2,1)S(1)} all-to-all(bf16[2,8,1024]{2,0,1:T(2,128)(2,1)S(1)} %copy.33), channel_id=1, replica_groups=mesh['tp'=8,'dp'=4] {'tp'}, dimensions={1} | all-to-all | bytes 65536 | tf_op jit(solution)/shard_map/all_to_all | solution.py:113
  113.6 0.0 all-gather.2.cloned.1.call-done
  113.6 2.2 %convolution_convert_fusion = bf16[16,1024]{1,0:T(8,128)(2,1)S(1)} fusion(bf16[16,1024]{1,0:T(8,128)(2,1)S(1)} %all_to_all.14, bf16[1024,1024]{1,0:T(8,128)(2,1)} %all-gather.2.cloned.1.call-done), kind=kOutput, calls=%fused_computation.6 | convolution fusion | flops 33570816 | bytes 2162688 | tf_op jit(solution)/shard_map/dot_general | solution.py:115
  115.8 0.8 copy.38
  116.7 0.0 reduce-scatter.7.cloned.1.call-update
  116.7 32.9 %reduce-scatter.7.cloned.1.call-done = bf16[128,16]{1,0:T(8,128)(2,1)} async-done(((bf16[1024,16]{1,0:T(8,128)(2,1)}), bf16[128,16]{1,0:T(8,128)(2,1)}) %reduce-scatter.7.cloned.1.call-update) | async-done | bytes 4112
  149.6 0.8 copy.39
  150.4 0.6 convert_multiply_fusion.2
  (13 shorter events, 0.1 us)
Async XLA Ops:
  7.4 0.7 copy-start
  7.4 92.0 %reduce-scatter.5.cloned.1.call-start = ((), (), s32[]{:S(2)}) async-start(), calls=%async_computation.3 | async-start | bytes 8257536 | tf_op jit(solution)/shard_map/reduce_scatter | solution.py:101
  13.5 6.4 %copy-start.1 = (bf16[16,512,512]{2,1,0:T(8,128)(2,1)S(1)}, bf16[16,512,512]{2,1,0:T(8,128)(2,1)}, u32[]{:S(2)}) copy-start(bf16[16,512,512]{2,1,0:T(8,128)(2,1)} %param.12) | copy-start | bytes 25165828
  19.9 3.4 %copy-start.2 = (bf16[16,512,512]{2,1,0:T(8,128)(2,1)S(1)}, bf16[16,512,512]{2,1,0:T(8,128)(2,1)}, u32[]{:S(2)}) copy-start(bf16[16,512,512]{2,1,0:T(8,128)(2,1)} %param.11) | copy-start | bytes 25165828
  29.5 1.0 copy-start.3
  29.5 17.4 %copy-start.4 = (f32[8192]{0:T(1024)S(1)}, f32[8192]{0:T(1024)}, u32[]{:S(2)}) copy-start(f32[8192]{0:T(1024)} %param.19) | copy-start | bytes 98308
  29.5 17.4 %copy-start.5 = (f32[8192]{0:T(1024)S(1)}, f32[8192]{0:T(1024)}, u32[]{:S(2)}) copy-start(f32[8192]{0:T(1024)} %param.20) | copy-start | bytes 98308
  29.5 17.5 %copy-start.6 = (s32[16]{0:T(128)S(1)}, s32[16]{0:T(128)}, u32[]{:S(2)}) copy-start(s32[16]{0:T(128)} %param.14) | copy-start | bytes 196
  29.6 84.0 %all-gather.2.cloned.1.call-start = ((), (), s32[]{:S(2)}) async-start(), calls=%async_computation.4 | async-start | bytes 2621440 | tf_op jit(solution)/shard_map/all_gather | solution.py:117
  46.9 102.7 %reduce-scatter.7.cloned.1.call-start = ((), (), s32[]{:S(2)}) async-start(), calls=%async_computation.5 | async-start | bytes 294912
Sparse Core Ops, SparseCore 0:
  29.7 69.6 reduce-scatter.4
  116.8 32.7 reduce-scatter.6
Sparse Core Ops, SparseCore 1:
  47.0 44.9 all-gather.1
where the time goes:
time: 159 us; the launch traced here: 158 us
  waiting for transfers between devices  85.1 us (54%)
  matrix products  23.6 us (15%)
  blocking collectives  22.5 us (14%)
  between operations  15 us (9%)
  other arithmetic  6.89 us (4%)
  local copies, waits for them, and re-layouts  5.24 us (3%)
    reduce_scatter x1, waiting for transfers between devices, body(): lax.psum_scatter(jnp.concatenate([left_part, right_q, right_v], axis=-1)....  52.2 us
    unnamed x4, waiting for transfers between devices  32.9 us
    psum x1, blocking collectives, body(): target_total = lax.psum(target_sq, 'tp')  15.1 us
    all_to_all x1, blocking collectives, body(): lax.all_to_all(own_train, 'tp', split_axis=1, concat_axis=0, tiled=True)  7.37 us
    dot_general x1, matrix products, body(): jnp.einsum('esd,dc->esc', value_output_cotangent, w_value, preferred_elem...  6.4 us
    dot_general x4, matrix products, outer_sum(): jnp.einsum(pattern, left_side, right_side, precision=lax.Precision.HIGHEST)  5.09 us
    unnamed x18, local copies, waits for them, and re-layouts  4.05 us
    concatenate x1, other arithmetic, body(): jnp.concatenate([left_part, right_q, right_v], axis=-1).astype(jnp.bfloat16)  3.35 us
  transfers between devices with their start and end apart: 3, of which 2 were waited for; matrix products, arithmetic and copies ran while one was open for 5% of the time, Pallas kernels for 0%

commit v1 on v0

--- a/solution.py
+++ b/solution.py
@@ -108,7 +108,11 @@
     features = compute_features(token_sums, own_mask, "es", rank_cols)
     update = adam_update(features, projected_first_moment, projected_second_moment)
     squares = jnp.sum(update * update, axis=1)
-    target_total = lax.psum(target_sq, "tp")
+    target_total = target_sq
+    for hop in (1, 2, 4):
+        target_total = target_total + lax.ppermute(
+            target_total, "tp", [(dev, dev ^ hop) for dev in range(8)]
+        )
     own_train = (update * lax.rsqrt(squares + 1e-06)[:, None]).astype(jnp.bfloat16)
     train_rows = lax.all_to_all(own_train, "tp", split_axis=1, concat_axis=0, tiled=True)
     unit_targets = (target_float * lax.rsqrt(target_total + 1e-06)[:, None]).astype(jnp.bfloat16)

time: 159 us -> 159 us (level)
  blocking collectives: 22.5 us -> 7.37 us
  waiting for transfers between devices: 85.1 us -> 94.9 us
  starting transfers between devices: 0.09 us -> 5.46 us
    psum x1 -> x0, blocking collectives: 15.1 us -> none  [body(): target_total = lax.psum(target_sq, 'tp')]
    reduce_scatter x1, waiting for transfers between devices: 52.2 us -> 58 us  [body(): lax.psum_scatter(jnp.concatenate([left_part, right_q, right_v], axis=-1)....]
    ppermute x0 -> x3, starting transfers between devices: none -> 5.37 us  [body(): lax.ppermute(target_total, 'tp', [(dev, dev ^ hop) for dev in range(8)])]
    ppermute x0 -> x3, waiting for transfers between devices: none -> 3.91 us  [body(): lax.ppermute(target_total, 'tp', [(dev, dev ^ hop) for dev in range(8)])]
  transfers between devices with their start and end apart: 3 -> 6, of which waited for: 2 -> 5; matrix products, arithmetic and copies ran while one was open for 5% -> 5% of each run, Pallas kernels for 0% -> 0%
where the time goes in v1:
time: 159 us; the launch traced here: 158 us
  waiting for transfers between devices  94.9 us (60%)
  matrix products  23.6 us (15%)
  between operations  15 us (9%)
  blocking collectives  7.37 us (5%)
  other arithmetic  6.87 us (4%)
  starting transfers between devices  5.46 us (3%)
  local copies, waits for them, and re-layouts  5.25 us (3%)
    reduce_scatter x1, waiting for transfers between devices, body(): lax.psum_scatter(jnp.concatenate([left_part, right_q, right_v], axis=-1)....  58 us
    unnamed x4, waiting for transfers between devices  32.9 us
    all_to_all x1, blocking collectives, body(): lax.all_to_all(own_train, 'tp', split_axis=1, concat_axis=0, tiled=True)  7.37 us
    dot_general x1, matrix products, body(): jnp.einsum('esd,dc->esc', value_output_cotangent, w_value, preferred_elem...  6.4 us
    ppermute x3, starting transfers between devices, body(): lax.ppermute(target_total, 'tp', [(dev, dev ^ hop) for dev in range(8)])  5.37 us
    dot_general x4, matrix products, outer_sum(): jnp.einsum(pattern, left_side, right_side, precision=lax.Precision.HIGHEST)  5.09 us
    unnamed x18, local copies, waits for them, and re-layouts  4.06 us
    ppermute x3, waiting for transfers between devices, body(): lax.ppermute(target_total, 'tp', [(dev, dev ^ hop) for dev in range(8)])  3.91 us
  transfers between devices with their start and end apart: 6, of which 5 were waited for; matrix products, arithmetic and copies ran while one was open for 5% of the time, Pallas kernels for 0%

profile of v1, /device:TPU:0, one launch (start us, length us, event | category | flops | bytes accessed | tf_op | source)
XLA Modules:
  0.0 158.5 jit_solution(494498293146888636)
XLA Ops:
  7.4 0.0 copy-start
  7.4 0.7 copy-done
  8.1 1.0 convolution_convert_fusion.1
  9.1 1.0 convolution_convert_fusion.2
  10.1 1.0 convolution_convert_fusion.3
  11.2 1.1 convolution_convert_fusion.4
  12.2 1.0 fusion.41
  13.2 0.1 copy.41
  13.4 0.1 copy.40
  13.5 0.0 copy-start.1
  13.5 6.4 %convert_bitcast_fusion.1 = bf16[16,512,144]{1,2,0:T(8,128)(2,1)S(1)} fusion(bf16[16,512,512]{2,1,0:T(8,128)(2,1)} %param.13, bf16[512,16]{0,1:T(8,128)(2,1)S(1)} %convolution_convert_fusion.1, bf16[512,128]{0,1:T(8,128)(2,1)S(1)} %bitcast.53), kind=kOutput, calls=%fused_computation.2 | convolution fusion | flops 1209434112 | bytes 10895360 | tf_op jit(solution)/shard_map/esd,dc->esc/dot_general | solution.py:98
  19.9 0.0 copy-done.1
  19.9 0.0 copy-start.2
  19.9 2.9 %convert_bitcast_fusion.2 = bf16[16,512,144]{1,2,0:T(8,128)(2,1)S(1)} fusion(bf16[16,512,512]{2,1,0:T(8,128)(2,1)S(1)} %copy-done.1, bf16[512,16]{0,1:T(8,128)(2,1)S(1)} %convolution_convert_fusion.2, bf16[512,128]{0,1:T(8,128)(2,1)S(1)} %bitcast.54), kind=kOutput, calls=%fused_computation.3 | convolution fusion | flops 1209434112 | bytes 10895360 | tf_op jit(solution)/shard_map/esd,dc->esc/dot_general | solution.py:95
  22.8 0.5 copy-done.2
  23.3 2.9 %convert_bitcast_fusion = bf16[16,512,160]{1,2,0:T(8,128)(2,1)S(1)} fusion(bf16[16,512,512]{2,1,0:T(8,128)(2,1)S(1)} %copy-done.2, bf16[512,128]{0,1:T(8,128)(2,1)S(1)} %bitcast.56, bf16[512,16]{0,1:T(8,128)(2,1)S(1)} %convolution_convert_fusion.3, bf16[512,16]{0,1:T(8,128)(2,1)S(1)} %convolution_convert_fusion.4), kind=kOutput, calls=%fused_computation.1 | convolution fusion | flops 1343979520 | bytes 11173888 | tf_op jit(solution)/shard_map/esd,dc->esc/dot_general | solution.py:94
  26.2 3.3 %pad_maximum_fusion = bf16[16,512,448]{1,2,0:T(8,128)(2,1)} fusion(bf16[16,512,144]{1,2,0:T(8,128)(2,1)S(1)} %convert_bitcast_fusion.1, bf16[16,512,144]{1,2,0:T(8,128)(2,1)S(1)} %convert_bitcast_fusion.2, bf16[16,512,160]{1,2,0:T(8,128)(2,1)S(1)} %convert_bitcast_fusion), kind=kLoop, calls=%fused_computation | loop fusion | flops 22020096 | bytes 14680064 | tf_op jit(solution)/shard_map/concatenate | solution.py:102
  29.5 0.0 reduce-scatter.5.cloned.1.call-update
  29.5 0.0 all-gather.2.cloned.1.call-start
  29.6 1.0 copy-done.3
  30.5 0.2 fusion
  30.7 0.5 collective-permute-start
  31.2 0.8 collective-permute-done
  32.1 2.8 %collective-permute-start.1 = (f32[256]{0:T(256)S(1)}, f32[256]{0:T(256)S(1)}, u32[]{:S(2)}, u32[]{:S(2)}) collective-permute-start(f32[256]{0:T(256)S(1)} %add.95), channel_id=1, source_target_pairs={{0,8},{4,12},{8,0},{12,4},{16,24},{20,28},{24,16},{28,20},{1,9},{5... | collective-permute-start | bytes 3080 | tf_op jit(solution)/shard_map/ppermute | solution.py:113
  34.9 1.5 collective-permute-done.1
  36.4 2.1 %collective-permute-start.2 = (f32[256]{0:T(256)S(1)}, f32[256]{0:T(256)S(1)}, u32[]{:S(2)}, u32[]{:S(2)}) collective-permute-start(f32[256]{0:T(256)S(1)} %add.96), channel_id=1, source_target_pairs={{0,16},{4,20},{8,24},{12,28},{16,0},{20,4},{24,8},{28,12},{1,17},{... | collective-permute-start | bytes 3080 | tf_op jit(solution)/shard_map/ppermute | solution.py:113
  38.5 1.5 collective-permute-done.2
  40.0 1.0 fusion.1
  41.0 0.0 all-gather.2.cloned.1.call-update
  41.0 0.0 reduce-scatter.7.cloned.1.call-start
  41.2 0.1 dynamic-slice
  41.3 0.1 compare_convert_fusion
  41.3 58.0 %reduce-scatter.5.cloned.1.call-done = bf16[2,512,448]{1,2,0:T(8,128)(2,1)} async-done(((bf16[16,512,448]{1,2,0:T(8,128)(2,1)}), bf16[2,512,448]{1,2,0:T(8,128)(2,1)}) %reduce-scatter.5.cloned.1.call-update) | async-done | bytes 917520 | tf_op jit(solution)/shard_map/reduce_scatter | solution.py:101
  99.4 1.4 convert_element_type.39
  100.8 1.3 convolution_bitcast_fusion.3
  102.1 1.3 convolution_bitcast_fusion.2
  103.3 1.3 convolution_bitcast_fusion.1
  104.6 1.3 convolution_bitcast_fusion
  105.9 0.2 fusion.33
  106.1 0.1 fusion.32
  106.2 7.4 %all_to_all.16 = bf16[2,8,1024]{2,0,1:T(2,128)(2,1)S(1)} all-to-all(bf16[2,8,1024]{2,0,1:T(2,128)(2,1)S(1)} %copy.33), channel_id=1, replica_groups=mesh['tp'=8,'dp'=4] {'tp'}, dimensions={1} | all-to-all | bytes 65536 | tf_op jit(solution)/shard_map/all_to_all | solution.py:117
  113.6 0.0 all-gather.2.cloned.1.call-done
  113.6 2.2 %convolution_convert_fusion = bf16[16,1024]{1,0:T(8,128)(2,1)S(1)} fusion(bf16[16,1024]{1,0:T(8,128)(2,1)S(1)} %all_to_all.14, bf16[1024,1024]{1,0:T(8,128)(2,1)} %all-gather.2.cloned.1.call-done), kind=kOutput, calls=%fused_computation.6 | convolution fusion | flops 33570816 | bytes 2162688 | tf_op jit(solution)/shard_map/dot_general | solution.py:119
  115.9 0.9 copy.38
  116.7 0.0 reduce-scatter.7.cloned.1.call-update
  116.7 32.9 %reduce-scatter.7.cloned.1.call-done = bf16[128,16]{1,0:T(8,128)(2,1)} async-done(((bf16[1024,16]{1,0:T(8,128)(2,1)}), bf16[128,16]{1,0:T(8,128)(2,1)}) %reduce-scatter.7.cloned.1.call-update) | async-done | bytes 4112
  149.6 0.8 copy.39
  150.4 0.6 convert_multiply_fusion.2
  (20 shorter events, 0.1 us)
Async XLA Ops:
  7.4 0.7 copy-start
  7.4 92.0 %reduce-scatter.5.cloned.1.call-start = ((), (), s32[]{:S(2)}) async-start(), calls=%async_computation.3 | async-start | bytes 8257536 | tf_op jit(solution)/shard_map/reduce_scatter | solution.py:101
  13.5 6.4 %copy-start.1 = (bf16[16,512,512]{2,1,0:T(8,128)(2,1)S(1)}, bf16[16,512,512]{2,1,0:T(8,128)(2,1)}, u32[]{:S(2)}) copy-start(bf16[16,512,512]{2,1,0:T(8,128)(2,1)} %param.12) | copy-start | bytes 25165828
  19.9 3.4 %copy-start.2 = (bf16[16,512,512]{2,1,0:T(8,128)(2,1)S(1)}, bf16[16,512,512]{2,1,0:T(8,128)(2,1)}, u32[]{:S(2)}) copy-start(bf16[16,512,512]{2,1,0:T(8,128)(2,1)} %param.11) | copy-start | bytes 25165828
  29.5 1.0 copy-start.3
  29.5 11.6 %copy-start.4 = (f32[8192]{0:T(1024)S(1)}, f32[8192]{0:T(1024)}, u32[]{:S(2)}) copy-start(f32[8192]{0:T(1024)} %param.19) | copy-start | bytes 98308
  29.5 11.6 %copy-start.5 = (f32[8192]{0:T(1024)S(1)}, f32[8192]{0:T(1024)}, u32[]{:S(2)}) copy-start(f32[8192]{0:T(1024)} %param.20) | copy-start | bytes 98308
  29.5 11.7 %copy-start.6 = (s32[16]{0:T(128)S(1)}, s32[16]{0:T(128)}, u32[]{:S(2)}) copy-start(s32[16]{0:T(128)} %param.14) | copy-start | bytes 196
  29.5 84.1 %all-gather.2.cloned.1.call-start = ((), (), s32[]{:S(2)}) async-start(), calls=%async_computation.4 | async-start | bytes 2621440 | tf_op jit(solution)/shard_map/all_gather | solution.py:121
  30.7 1.3 collective-permute-start
  32.1 4.4 %collective-permute-start.1 = (f32[256]{0:T(256)S(1)}, f32[256]{0:T(256)S(1)}, u32[]{:S(2)}, u32[]{:S(2)}) collective-permute-start(f32[256]{0:T(256)S(1)} %add.95), channel_id=1, source_target_pairs={{0,8},{4,12},{8,0},{12,4},{16,24},{20,28},{24,16},{28,20},{1,9},{5... | collective-permute-start | bytes 3080 | tf_op jit(solution)/shard_map/ppermute | solution.py:113
  36.4 3.6 %collective-permute-start.2 = (f32[256]{0:T(256)S(1)}, f32[256]{0:T(256)S(1)}, u32[]{:S(2)}, u32[]{:S(2)}) collective-permute-start(f32[256]{0:T(256)S(1)} %add.96), channel_id=1, source_target_pairs={{0,16},{4,20},{8,24},{12,28},{16,0},{20,4},{24,8},{28,12},{1,17},{... | collective-permute-start | bytes 3080 | tf_op jit(solution)/shard_map/ppermute | solution.py:113
  41.0 108.6 %reduce-scatter.7.cloned.1.call-start = ((), (), s32[]{:S(2)}) async-start(), calls=%async_computation.5 | async-start | bytes 294912
Sparse Core Ops, SparseCore 0:
  29.7 69.6 reduce-scatter.4
  116.9 32.6 reduce-scatter.6
Sparse Core Ops, SparseCore 1:
  41.1 47.3 all-gather.1
